TPU v7x, 32 devices: a whole 2x2x4 slice. The times are simulated.
32 devices in a mesh: fsdp: 8 (over z, x), dp: 4 (over y, core).
Axes of the slice: x: 2, y: 2, z: 4, core: 2. Of those that a mesh axis runs over, the one named last changes fastest.
Arguments:
- hidden: bfloat16 [2, 32, 384, 1536], P(None, ('fsdp', 'dp')), may hold values from -6 to 6
- teacher: bfloat16 [2, 32, 384, 1536], P(None, ('fsdp', 'dp')), may hold values from -6 to 6
- cotangent: bfloat16 [2, 32, 384, 1536], P(None, ('fsdp', 'dp')), may hold values from -6.3329935e-07 to 6.3329935e-07
- valid_mask: int32 [2, 32, 384], P(None, ('fsdp', 'dp')), may hold values from 0 to 1, as said below
- blocks: int32 [2, 32, 384], P(None, ('fsdp', 'dp')), may hold values from 0 to 2, never falling along the last dimension, each value on 1 to 256 neighbouring positions
- buckets: int32 [384, 384], replicated, may hold values from 0 to 31
- first_gain: bfloat16 [1536], P(('fsdp', 'dp')), may hold values from 0.25 to 1.75
- query_weight: bfloat16 [1536, 768], P('fsdp', 'dp'), may hold values from -0.0390625 to 0.0390625
- key_weight: bfloat16 [1536, 768], P('fsdp', 'dp'), may hold values from -0.15625 to 0.15625
- value_weight: bfloat16 [1536, 768], P('fsdp', 'dp'), may hold values from -0.15625 to 0.15625
- output_weight: bfloat16 [1536, 768], P('fsdp', 'dp'), may hold values from -1.25 to 1.25
- second_gain: bfloat16 [1536], P(('fsdp', 'dp')), may hold values from 0.25 to 1.75
- gate_weight: bfloat16 [1536, 3968], P('fsdp', 'dp'), may hold values from -0.15625 to 0.15625
- up_weight: bfloat16 [1536, 3968], P('fsdp', 'dp'), may hold values from -0.15625 to 0.15625
- down_weight: bfloat16 [1536, 3968], P('fsdp', 'dp'), may hold values from -0.1875 to 0.1875
- bias_table: bfloat16 [32, 12], replicated, may hold values from -5 to 5
Outputs:
- layer_output: bfloat16 [2, 32, 384, 1536], P(None, ('fsdp', 'dp'))
- loss_value: float32 [], replicated
- hidden_grad: bfloat16 [2, 32, 384, 1536], P(None, ('fsdp', 'dp'))
- first_gain_grad: float32 [1536], P(('fsdp', 'dp'))
- query_grad: float32 [1536, 768], P('fsdp', 'dp')
- key_grad: float32 [1536, 768], P('fsdp', 'dp')
- value_grad: float32 [1536, 768], P('fsdp', 'dp')
- output_grad: float32 [1536, 768], P('fsdp', 'dp')
- second_gain_grad: float32 [1536], P(('fsdp', 'dp'))
- gate_grad: float32 [1536, 3968], P('fsdp', 'dp')
- up_grad: float32 [1536, 3968], P('fsdp', 'dp')
- down_grad: float32 [1536, 3968], P('fsdp', 'dp')
- bias_grad: float32 [32, 12], replicated
Inputs may be any that keep to these rules, and one draw needn't show every extreme that they name: `valid_mask`: 1 marks a valid token. `blocks`: never falls along a sequence; every block number up to the largest occurs, each block has 1 to 256 positions and some block has exactly 256.
All inputs are finite; a program needn't handle non-finite values.
Results may differ from a plain program's by a relative error of at most 0.013.
The roundings to bfloat16 on the way count: a program that leaves them out, or rounds other values in their place, can miss the bound.
Values may be sent and summed in bfloat16 or wider, within the bound.
A program may use at most 320 MiB of HBM per device.

v0:
```python
import jax
import jax.numpy as jnp
from jax import lax
from jax.sharding import PartitionSpec as P

EPS = 1e-06
NEG = -1000000000.0
HIGH = lax.Precision.HIGHEST


def times_rows(former, latter):
    return jnp.dot(former, latter, preferred_element_type=jnp.float32)


def times_transpose(former, latter):
    return lax.dot_general(
        former, latter, (((1,), (1,)), ((), ())), preferred_element_type=jnp.float32
    )


def over_tokens(former, latter):
    return lax.dot_general(
        former, latter, (((0,), (0,)), ((), ())), preferred_element_type=jnp.float32
    )


def assemble(gathered, fsdp_count, dp_count):
    row_block = gathered.shape[0] // (fsdp_count * dp_count)
    col_block = gathered.shape[1]
    shaped = gathered.reshape(fsdp_count, dp_count, row_block, col_block)
    return jnp.transpose(shaped, (0, 2, 1, 3)).reshape(fsdp_count * row_block, dp_count * col_block)


def disperse(gradient, fsdp_count, dp_count):
    row_block = gradient.shape[0] // fsdp_count
    col_block = gradient.shape[1] // dp_count
    shaped = gradient.reshape(fsdp_count, row_block, dp_count, col_block)
    return jnp.transpose(shaped, (0, 2, 1, 3)).reshape(fsdp_count * dp_count * row_block, col_block)


def norm_forward(inputs, norm_gain):
    row_scale = lax.rsqrt(jnp.mean(inputs * inputs, axis=-1, keepdims=True) + EPS)
    return (inputs * row_scale * norm_gain, row_scale)


def norm_backward(inputs, row_scale, norm_gain, upstream):
    scaled = upstream * norm_gain
    gain_grad = jnp.sum(upstream * inputs * row_scale, axis=0)
    mean_term = jnp.mean(scaled * inputs, axis=-1, keepdims=True)
    return (
        row_scale * scaled - inputs * (row_scale * row_scale * row_scale) * mean_term,
        gain_grad,
    )


def gelu_tanh(values_in):
    return jax.nn.gelu(values_in, approximate=True)


def masked_scores(queries, key_heads, position_bias, allowed):
    products = jnp.einsum("qhd,khd->hqk", queries, key_heads, preferred_element_type=jnp.float32)
    return jnp.where(allowed[None], products + position_bias, NEG)


def body(
    hidden,
    teacher,
    cotangent,
    valid_mask,
    blocks,
    buckets,
    first_gain,
    query_weight,
    key_weight,
    value_weight,
    output_weight,
    second_gain,
    gate_weight,
    up_weight,
    down_weight,
    bias_table,
):
    fsdp_count = lax.axis_size("fsdp")
    dp_count = lax.axis_size("dp")
    micro_count = hidden.shape[0]
    seq_len = hidden.shape[2]
    model_width = hidden.shape[3]
    bucket_count = bias_table.shape[0]
    head_count = bias_table.shape[1]
    scale_factor = jnp.float32(
        float(micro_count * lax.axis_size(("fsdp", "dp")) * hidden.shape[1] * seq_len * model_width)
    )
    valid_float = valid_mask.astype(jnp.float32)
    valid_total = lax.psum(jnp.sum(valid_float), ("fsdp", "dp"))
    places = lax.broadcasted_iota(jnp.int32, (1, 1, bucket_count), 2)
    onehot = (buckets[:, :, None] == places).astype(jnp.float32)
    position_bias = jnp.einsum(
        "qkb,bh->hqk", onehot, bias_table.astype(jnp.float32), precision=HIGH
    )
    onehot_low = onehot.astype(jnp.bfloat16)
    rows_iota = lax.broadcasted_iota(jnp.int32, (seq_len, seq_len), 0)
    cols_iota = lax.broadcasted_iota(jnp.int32, (seq_len, seq_len), 1)
    diagonal = rows_iota == cols_iota

    def rebuild(gathered):
        return (gathered[0],) + tuple(
            (assemble(matrix, fsdp_count, dp_count) for matrix in gathered[1:])
        )

    def spread_out(grads):
        return (
            (grads[0],)
            + tuple((disperse(matrix, fsdp_count, dp_count) for matrix in grads[1:5]))
            + (grads[5],)
            + tuple((disperse(matrix, fsdp_count, dp_count) for matrix in grads[6:]))
        )

    outputs_list = []
    input_grads = []
    squares = jnp.float32(0.0)
    table_grad = jnp.zeros((bucket_count, head_count), jnp.float32)
    totals = None
    for step_index in range(micro_count):
        inputs = hidden[step_index, 0].astype(jnp.float32)
        target = teacher[step_index, 0].astype(jnp.float32)
        upstream = cotangent[step_index, 0].astype(jnp.float32)
        token_valid = valid_float[step_index, 0]
        block_ids = blocks[step_index, 0]
        allowed = (block_ids[None, :] <= block_ids[:, None]) & (
            valid_mask[step_index, 0][None, :] == 1
        ) | diagonal
        first_block = rebuild(
            (
                lax.all_gather(first_gain, ("fsdp", "dp"), axis=0, tiled=True),
                lax.all_gather(query_weight, ("fsdp", "dp"), axis=0, tiled=True),
                lax.all_gather(key_weight, ("fsdp", "dp"), axis=0, tiled=True),
                lax.all_gather(value_weight, ("fsdp", "dp"), axis=0, tiled=True),
                lax.all_gather(output_weight, ("fsdp", "dp"), axis=0, tiled=True),
            )
        )
        gain_one = first_block[0].astype(jnp.float32)
        normed_full, scale_one = norm_forward(inputs, gain_one)
        normed_one = normed_full.astype(jnp.bfloat16)
        head_size = first_block[1].shape[1] // head_count
        head_split = (seq_len, head_count, head_size)
        queries = times_rows(normed_one, first_block[1]).astype(jnp.bfloat16).reshape(head_split)
        key_heads = times_rows(normed_one, first_block[2]).astype(jnp.bfloat16).reshape(head_split)
        value_heads = (
            times_rows(normed_one, first_block[3]).astype(jnp.bfloat16).reshape(head_split)
        )
        scores = masked_scores(queries, key_heads, position_bias, allowed)
        row_max = jnp.max(scores, axis=-1, keepdims=True)
        exponent = jnp.exp(scores - row_max)
        row_total = jnp.sum(exponent, axis=-1, keepdims=True)
        log_total = row_max + jnp.log(row_total)
        softmax_low = (exponent / row_total).astype(jnp.bfloat16)
        attended = jnp.einsum(
            "hqk,khd->qhd", softmax_low, value_heads, preferred_element_type=jnp.float32
        )
        attended = attended.astype(jnp.bfloat16).reshape(seq_len, head_count * head_size)
        middle = inputs + times_transpose(attended, first_block[4])
        second_block = rebuild(
            (
                lax.all_gather(second_gain, ("fsdp", "dp"), axis=0, tiled=True),
                lax.all_gather(gate_weight, ("fsdp", "dp"), axis=0, tiled=True),
                lax.all_gather(up_weight, ("fsdp", "dp"), axis=0, tiled=True),
                lax.all_gather(down_weight, ("fsdp", "dp"), axis=0, tiled=True),
            )
        )
        gain_two = second_block[0].astype(jnp.float32)
        normed_mid, scale_two = norm_forward(middle, gain_two)
        normed_two = normed_mid.astype(jnp.bfloat16)
        gate_pre = times_rows(normed_two, second_block[1])
        up_pre = times_rows(normed_two, second_block[2])
        gate_act, gelu_pullback = jax.vjp(gelu_tanh, gate_pre)
        hidden_act = (gate_act * up_pre).astype(jnp.bfloat16)
        layer_full = middle + times_transpose(hidden_act, second_block[3])
        outputs_list.append(layer_full.astype(jnp.bfloat16))
        residual_gap = layer_full - target
        weighted_gap = token_valid[:, None] * residual_gap
        squares = squares + jnp.sum(weighted_gap * residual_gap)
        grad_out = scale_factor * upstream + scale_factor * (
            2.0 * weighted_gap / (valid_total * model_width)
        )
        back_second = rebuild(
            (
                lax.all_gather(second_gain, ("fsdp", "dp"), axis=0, tiled=True),
                lax.all_gather(gate_weight, ("fsdp", "dp"), axis=0, tiled=True),
                lax.all_gather(up_weight, ("fsdp", "dp"), axis=0, tiled=True),
                lax.all_gather(down_weight, ("fsdp", "dp"), axis=0, tiled=True),
            )
        )
        grad_ffn = grad_out.astype(jnp.bfloat16)
        down_part = over_tokens(grad_ffn, hidden_act)
        grad_hidden_act = times_rows(grad_ffn, back_second[3])
        grad_gate = gelu_pullback(grad_hidden_act * up_pre)[0].astype(jnp.bfloat16)
        grad_up = (grad_hidden_act * gate_act).astype(jnp.bfloat16)
        gate_part = over_tokens(normed_two, grad_gate)
        up_part = over_tokens(normed_two, grad_up)
        grad_normed_two = times_transpose(grad_gate, back_second[1]) + times_transpose(
            grad_up, back_second[2]
        )
        middle_term, gain_two_part = norm_backward(
            middle, scale_two, back_second[0].astype(jnp.float32), grad_normed_two
        )
        grad_middle = grad_out + middle_term
        grad_attn = grad_middle.astype(jnp.bfloat16)
        back_first = rebuild(
            (
                lax.all_gather(first_gain, ("fsdp", "dp"), axis=0, tiled=True),
                lax.all_gather(query_weight, ("fsdp", "dp"), axis=0, tiled=True),
                lax.all_gather(key_weight, ("fsdp", "dp"), axis=0, tiled=True),
                lax.all_gather(value_weight, ("fsdp", "dp"), axis=0, tiled=True),
                lax.all_gather(output_weight, ("fsdp", "dp"), axis=0, tiled=True),
            )
        )
        output_part = over_tokens(grad_attn, attended)
        grad_attended = (
            times_rows(grad_attn, back_first[4]).astype(jnp.bfloat16).reshape(head_split)
        )
        scores_again = masked_scores(queries, key_heads, position_bias, allowed)
        softmax_again = jnp.exp(scores_again - log_total)
        grad_probs = jnp.einsum(
            "qhd,khd->hqk", grad_attended, value_heads, preferred_element_type=jnp.float32
        )
        grad_scores = softmax_again * (
            grad_probs - jnp.sum(softmax_again * grad_probs, axis=-1, keepdims=True)
        )
        grad_scores = grad_scores.astype(jnp.bfloat16)
        table_grad = table_grad + jnp.einsum(
            "hqk,qkb->bh", grad_scores, onehot_low, preferred_element_type=jnp.float32
        )
        flat_width = head_count * head_size
        grad_queries = (
            jnp.einsum("hqk,khd->qhd", grad_scores, key_heads, preferred_element_type=jnp.float32)
            .astype(jnp.bfloat16)
            .reshape(seq_len, flat_width)
        )
        grad_keys = (
            jnp.einsum("hqk,qhd->khd", grad_scores, queries, preferred_element_type=jnp.float32)
            .astype(jnp.bfloat16)
            .reshape(seq_len, flat_width)
        )
        grad_values = (
            jnp.einsum(
                "hqk,qhd->khd",
                softmax_again.astype(jnp.bfloat16),
                grad_attended,
                preferred_element_type=jnp.float32,
            )
            .astype(jnp.bfloat16)
            .reshape(seq_len, flat_width)
        )
        query_part = over_tokens(normed_one, grad_queries)
        key_part = over_tokens(normed_one, grad_keys)
        value_part = over_tokens(normed_one, grad_values)
        grad_normed_one = (
            times_transpose(grad_queries, back_first[1])
            + times_transpose(grad_keys, back_first[2])
            + times_transpose(grad_values, back_first[3])
        )
        input_term, gain_one_part = norm_backward(
            inputs, scale_one, back_first[0].astype(jnp.float32), grad_normed_one
        )
        input_grads.append((grad_middle + input_term).astype(jnp.bfloat16))
        step_set = spread_out(
            (
                gain_one_part,
                query_part,
                key_part,
                value_part,
                output_part,
                gain_two_part,
                gate_part,
                up_part,
                down_part,
            )
        )
        totals = step_set if totals is None else jax.tree.map(jnp.add, totals, step_set)
    shards = (
        lax.psum_scatter(totals[0], ("fsdp", "dp"), scatter_dimension=0, tiled=True),
        lax.psum_scatter(totals[1], ("fsdp", "dp"), scatter_dimension=0, tiled=True),
        lax.psum_scatter(totals[2], ("fsdp", "dp"), scatter_dimension=0, tiled=True),
        lax.psum_scatter(totals[3], ("fsdp", "dp"), scatter_dimension=0, tiled=True),
        lax.psum_scatter(totals[4], ("fsdp", "dp"), scatter_dimension=0, tiled=True),
        lax.psum_scatter(totals[5], ("fsdp", "dp"), scatter_dimension=0, tiled=True),
        lax.psum_scatter(totals[6], ("fsdp", "dp"), scatter_dimension=0, tiled=True),
        lax.psum_scatter(totals[7], ("fsdp", "dp"), scatter_dimension=0, tiled=True),
        lax.psum_scatter(totals[8], ("fsdp", "dp"), scatter_dimension=0, tiled=True),
    )
    total_squares, table_all = lax.psum((squares, table_grad), ("fsdp", "dp"))
    loss_value = total_squares / (valid_total * model_width)
    layer_output = jnp.stack(outputs_list)[:, None]
    hidden_grad = jnp.stack(input_grads)[:, None]
    return (
        layer_output,
        loss_value,
        hidden_grad,
        shards[0],
        shards[1],
        shards[2],
        shards[3],
        shards[4],
        shards[5],
        shards[6],
        shards[7],
        shards[8],
        table_all,
    )


def solution(mesh):
    in_specs = (
        P(None, ("fsdp", "dp"), None, None),
        P(None, ("fsdp", "dp"), None, None),
        P(None, ("fsdp", "dp"), None, None),
        P(None, ("fsdp", "dp"), None),
        P(None, ("fsdp", "dp"), None),
        P(),
        P(("fsdp", "dp")),
        P("fsdp", "dp"),
        P("fsdp", "dp"),
        P("fsdp", "dp"),
        P("fsdp", "dp"),
        P(("fsdp", "dp")),
        P("fsdp", "dp"),
        P("fsdp", "dp"),
        P("fsdp", "dp"),
        P(),
    )
    out_specs = (
        P(None, ("fsdp", "dp"), None, None),
        P(),
        P(None, ("fsdp", "dp"), None, None),
        P(("fsdp", "dp")),
        P("fsdp", "dp"),
        P("fsdp", "dp"),
        P("fsdp", "dp"),
        P("fsdp", "dp"),
        P(("fsdp", "dp")),
        P("fsdp", "dp"),
        P("fsdp", "dp"),
        P("fsdp", "dp"),
        P(),
    )
    return jax.shard_map(body, mesh=mesh, in_specs=in_specs, out_specs=out_specs, check_vma=False)
```

profile of v0, /device:TPU:0, one launch (start us, length us, event | category | flops | bytes accessed | tf_op | source)
XLA Modules:
  0.0 2003.4 jit_solution(12041364364537936734)
XLA Ops:
  13.3 42.2 %psum.22 = f32[]{:T(128)} all-reduce(f32[]{:T(128)} %convert_reduce_fusion), channel_id=1, replica_groups=mesh['fsdp'=8,'dp'=4] {'fsdp','dp'}, use_global_device_ids=true, to_apply=%region_12.13 | all-reduce | flops 1 | bytes 8 | tf_op jit(solution)/shard_map/psum | solution.py:94
  57.9 40.4 %all-reduce.5 = (bf16[1536]{0:T(1024)(128)(2,1)S(1)}, bf16[1536]{0:T(1024)(128)(2,1)S(1)}) all-reduce(bf16[1536]{0:T(1024)(128)(2,1)S(1)} %dynamic-update-slice, bf16[1536]{0:T(1024)(128)(2,1)S(1)} %dynamic-update-slice.1), channel_id=1, replica_groups=mesh['fsdp'=8,'dp'=4] {'fsdp','dp'}, use_global_device_ids=true, to_apply=%add | all-reduce | flops 3072 | bytes 12288
  114.5 6.1 reshape.535
  120.6 13.0 all-gather.12.cloned.1.call-done
  145.1 49.3 %all-gather.8.cloned.1.call-done = bf16[6144,192]{1,0:T(8,128)(2,1)} async-done(((bf16[192,192]{1,0:T(8,128)(2,1)}), bf16[6144,192]{1,0:T(8,128)(2,1)}) %all-gather.8.cloned.1.call-update) | async-done | bytes 2359312 | tf_op jit(solution)/shard_map/all_gather | solution.py:137
  205.9 49.1 %all-gather.14.cloned.1.call-done = bf16[6144,192]{1,0:T(8,128)(2,1)} async-done(((bf16[192,192]{1,0:T(8,128)(2,1)}), bf16[6144,192]{1,0:T(8,128)(2,1)}) %all-gather.14.cloned.1.call-update) | async-done | bytes 2359312 | tf_op jit(solution)/shard_map/all_gather | solution.py:138
  260.6 6.5 reshape.542
  298.9 7.2 fusion.119
  327.8 24.9 %all-gather.16.cloned.1.call-done = bf16[6144,992]{1,0:T(8,128)(2,1)} async-done(((bf16[192,992]{1,0:T(8,128)(2,1)}), bf16[6144,992]{1,0:T(8,128)(2,1)}) %all-gather.16.cloned.1.call-update) | async-done | bytes 12189712 | tf_op jit(solution)/shard_map/all_gather | solution.py:165
  352.6 15.6 copy.177
  368.2 25.0 %reshape.544 = bf16[1536,3968]{1,0:T(8,128)(2,1)} reshape(bf16[8,192,4,992]{3,2,1,0:T(4,128)(2,1)} %bitcast.396) | data formatting | bytes 24379392 | tf_op jit(solution)/shard_map/reshape | solution.py:31
  393.2 56.5 %all-gather.18.cloned.1.call-done = bf16[6144,992]{1,0:T(8,128)(2,1)} async-done(((bf16[192,992]{1,0:T(8,128)(2,1)}), bf16[6144,992]{1,0:T(8,128)(2,1)}) %all-gather.18.cloned.1.call-update) | async-done | bytes 12189712 | tf_op jit(solution)/shard_map/all_gather | solution.py:166
  449.7 15.6 copy.176
  465.3 25.2 %reshape.546 = bf16[1536,3968]{1,0:T(8,128)(2,1)} reshape(bf16[8,192,4,992]{3,2,1,0:T(4,128)(2,1)} %bitcast.397) | data formatting | bytes 24379392 | tf_op jit(solution)/shard_map/reshape | solution.py:31
  490.5 56.4 %all-gather.20.cloned.1.call-done = bf16[6144,992]{1,0:T(8,128)(2,1)} async-done(((bf16[192,992]{1,0:T(8,128)(2,1)}), bf16[6144,992]{1,0:T(8,128)(2,1)}) %all-gather.20.cloned.1.call-update) | async-done | bytes 12189712 | tf_op jit(solution)/shard_map/all_gather | solution.py:167
  546.8 15.6 copy.175
  562.5 25.0 %reshape.548 = bf16[1536,3968]{1,0:T(8,128)(2,1)} reshape(bf16[8,192,4,992]{3,2,1,0:T(4,128)(2,1)} %bitcast.398) | data formatting | bytes 24379392 | tf_op jit(solution)/shard_map/reshape | solution.py:31
  587.4 11.9 fusion.121
  599.3 11.8 fusion.122
  611.1 9.2 multiply_convert_fusion.4
  620.3 11.4 multiply_convert_fusion.5
  631.8 9.9 convolution_add_fusion.11
  641.7 13.7 fusion.74
  655.4 17.2 multiply_convert_fusion.3
  672.6 10.8 fusion.123
  683.4 15.5 multiply_convert_fusion.2
  698.9 10.8 fusion.125
  709.8 9.9 convolution_add_fusion.10
  719.7 19.5 multiply_reduce_fusion.2
  765.7 7.3 multiply_reduce_fusion.1
  773.0 7.1 multiply_convert_fusion.1
  837.8 14.0 fusion.106
  851.8 17.0 convolution_add_fusion
  868.8 32.5 %add.290 = f32[8,192,4,992]{3,2,1,0:T(4,128)} reshape(f32[1536,3968]{1,0:T(8,128)} %convolution_add_fusion) | data formatting | bytes 48758784 | tf_op jit(solution)/shard_map/add | solution.py:279
  901.4 25.3 %copy.140 = f32[8,4,192,992]{3,2,1,0:T(8,128)} copy(f32[8,4,192,992]{3,1,2,0:T(4,128)} %bitcast.393) | data formatting | bytes 48758784 | tf_op jit(solution)/shard_map/add | solution.py:279
  928.0 13.5 fusion.132
  941.5 17.0 convolution_add_fusion.1
  958.5 32.6 %add.286 = f32[8,192,4,992]{3,2,1,0:T(4,128)} reshape(f32[1536,3968]{1,0:T(8,128)} %convolution_add_fusion.1) | data formatting | bytes 48758784 | tf_op jit(solution)/shard_map/add | solution.py:279
  991.1 24.9 %copy.139 = f32[8,4,192,992]{3,2,1,0:T(8,128)} copy(f32[8,4,192,992]{3,1,2,0:T(4,128)} %bitcast.394) | data formatting | bytes 48758784 | tf_op jit(solution)/shard_map/add | solution.py:279
  1016.2 14.0 fusion.131
  1030.2 17.5 convolution_add_fusion.2
  1047.8 32.6 %add.282 = f32[8,192,4,992]{3,2,1,0:T(4,128)} reshape(f32[1536,3968]{1,0:T(8,128)} %convolution_add_fusion.2) | data formatting | bytes 48758784 | tf_op jit(solution)/shard_map/add | solution.py:279
  1080.3 25.2 %copy.138 = f32[8,4,192,992]{3,2,1,0:T(8,128)} copy(f32[8,4,192,992]{3,1,2,0:T(4,128)} %bitcast.395) | data formatting | bytes 48758784 | tf_op jit(solution)/shard_map/add | solution.py:279
  1116.8 40.0 %all-reduce.4 = (f32[]{:T(128)}, f32[1536]{0:T(1024)}, f32[1536]{0:T(1024)}, f32[32,12]{0,1:T(8,128)}) all-reduce(f32[]{:T(128)S(6)} %add.252, f32[1536]{0:T(1024)} %add.267, f32[1536]{0:T(1024)} %add.280, f32[32,12]{0,1:T(8,128)} %fusion.98), channel_id=1, replica_groups=mesh['fsdp'=8,'dp'=4] {'fsdp','dp'}, use_global_device_ids=true, to_apply=%region_10.11 | all-reduce | flops 3457 | bytes 27656 | tf_op jit(solution)/shard_map/psum | solution.py:291
  1169.0 69.7 %reduce-scatter.8.cloned.1.call-done = f32[192,192]{1,0:T(8,128)} async-done(((f32[6144,192]{1,0:T(8,128)}), f32[192,192]{1,0:T(8,128)}) %reduce-scatter.8.cloned.1.call-update) | async-done | bytes 147472 | tf_op jit(solution)/shard_map/reduce_scatter | solution.py:282
  1238.7 251.5 %reduce-scatter.20.cloned.1.call-done = f32[192,992]{1,0:T(8,128)} async-done(((f32[6144,992]{1,0:T(8,128)}), f32[192,992]{1,0:T(8,128)}) %reduce-scatter.20.cloned.1.call-update) | async-done | bytes 761872 | tf_op jit(solution)/shard_map/reduce_scatter | solution.py:289
  1490.2 253.2 %reduce-scatter.18.cloned.1.call-done = f32[192,992]{1,0:T(8,128)} async-done(((f32[6144,992]{1,0:T(8,128)}), f32[192,992]{1,0:T(8,128)}) %reduce-scatter.18.cloned.1.call-update) | async-done | bytes 761872 | tf_op jit(solution)/shard_map/reduce_scatter | solution.py:288
  1743.4 251.9 %reduce-scatter.16.cloned.1.call-done = f32[192,992]{1,0:T(8,128)} async-done(((f32[6144,992]{1,0:T(8,128)}), f32[192,992]{1,0:T(8,128)}) %reduce-scatter.16.cloned.1.call-update) | async-done | bytes 761872 | tf_op jit(solution)/shard_map/reduce_scatter | solution.py:287
  (333 shorter events, 212.0 us)
Async XLA Ops:
  7.2 96.6 %copy-start = (bf16[32,12]{0,1:T(8,128)(2,1)S(1)}, bf16[32,12]{0,1:T(8,128)(2,1)}, u32[]{:S(2)}) copy-start(bf16[32,12]{0,1:T(8,128)(2,1)} %param.31) | copy-start | bytes 2308
  7.2 94.3 %copy-start.75 = (s32[2,1,384]{2,1,0:T(1,128)S(1)}, s32[2,1,384]{2,1,0:T(1,128)}, u32[]{:S(2)}) copy-start(s32[2,1,384]{2,1,0:T(1,128)} %param.19) | copy-start | bytes 9220
  7.2 94.3 %copy-start.89 = (s32[2,1,384]{2,1,0:T(1,128)S(1)}, s32[2,1,384]{2,1,0:T(1,128)}, u32[]{:S(2)}) copy-start(s32[2,1,384]{2,1,0:T(1,128)} %param.20) | copy-start | bytes 9220
  7.2 94.3 %copy-start.4 = (bf16[2,1,384,1536]{3,2,1,0:T(8,128)(2,1)S(1)}, bf16[2,1,384,1536]{3,2,1,0:T(8,128)(2,1)}, u32[]{:S(2)}) copy-start(bf16[2,1,384,1536]{3,2,1,0:T(8,128)(2,1)} %param.16) | copy-start | bytes 7077892
  7.2 101.8 %all-gather.10.cloned.1.call-start = ((), (), s32[]{:S(2)}) async-start(), calls=%async_computation.8 | async-start | bytes 3244032 | tf_op jit(solution)/shard_map/all_gather | solution.py:135
  8.0 125.6 %all-gather.12.cloned.1.call-start = ((), (), s32[]{:S(2)}) async-start(), calls=%async_computation.9 | async-start | bytes 3244032 | tf_op jit(solution)/shard_map/all_gather | solution.py:136
  8.7 185.7 %all-gather.8.cloned.1.call-start = ((), (), s32[]{:S(2)}) async-start(), calls=%async_computation.7 | async-start | bytes 3244032 | tf_op jit(solution)/shard_map/all_gather | solution.py:137
  9.4 245.6 %all-gather.14.cloned.1.call-start = ((), (), s32[]{:S(2)}) async-start(), calls=%async_computation.10 | async-start | bytes 3244032 | tf_op jit(solution)/shard_map/all_gather | solution.py:138
  10.0 342.6 %all-gather.16.cloned.1.call-start = ((), (), s32[]{:S(2)}) async-start(), calls=%async_computation.11 | async-start | bytes 12976128 | tf_op jit(solution)/shard_map/all_gather | solution.py:165
  10.6 439.1 %all-gather.18.cloned.1.call-start = ((), (), s32[]{:S(2)}) async-start(), calls=%async_computation.12 | async-start | bytes 12976128 | tf_op jit(solution)/shard_map/all_gather | solution.py:166
  11.2 535.7 %all-gather.20.cloned.1.call-start = ((), (), s32[]{:S(2)}) async-start(), calls=%async_computation.13 | async-start | bytes 12976128 | tf_op jit(solution)/shard_map/all_gather | solution.py:167
  11.9 1157.1 %reduce-scatter.14.cloned.1.call-start = ((), (), s32[]{:S(2)}) async-start(), calls=%async_computation.17 | async-start | bytes 6488064 | tf_op jit(solution)/shard_map/reduce_scatter | solution.py:285
  98.9 228.4 %copy-start.69 = (f32[1536]{0:T(1024)}, f32[1536]{0:T(1024)S(1)}, u32[]{:S(2)}) copy-start(f32[1536]{0:T(1024)S(1)} %convert_element_type.234) | copy-start | bytes 18436
  102.7 172.8 %copy-start.76 = (f32[384]{0:T(512)}, f32[384]{0:T(512)S(1)}, u32[]{:S(2)}) copy-start(f32[384]{0:T(512)S(1)} %get-tuple-element.103) | copy-start | bytes 4612
  270.2 28.6 %copy-start.34 = (bf16[384,768]{0,1:T(8,128)(2,1)}, bf16[384,768]{0,1:T(8,128)(2,1)S(1)}, u32[]{:S(2)}) copy-start(bf16[384,768]{0,1:T(8,128)(2,1)S(1)} %copy.124) | copy-start | bytes 1769476
  275.5 23.4 %copy-start.36 = (bf16[384,768]{0,1:T(8,128)(2,1)}, bf16[384,768]{0,1:T(8,128)(2,1)S(1)}, u32[]{:S(2)}) copy-start(bf16[384,768]{0,1:T(8,128)(2,1)S(1)} %copy.123) | copy-start | bytes 1769476
  314.0 13.3 copy-start.11
  314.6 12.7 copy-start.82
  327.7 283.3 %copy-start.24 = (bf16[384,1536]{1,0:T(8,128)(2,1)}, bf16[384,1536]{1,0:T(8,128)(2,1)S(1)}, u32[]{:S(2)}) copy-start(bf16[384,1536]{1,0:T(8,128)(2,1)S(1)} %get-tuple-element.99) | copy-start | bytes 3538948
  327.7 292.6 %copy-start.28 = (bf16[384,1536]{1,0:T(8,128)(2,1)}, bf16[384,1536]{1,0:T(8,128)(2,1)S(1)}, u32[]{:S(2)}) copy-start(bf16[384,1536]{1,0:T(8,128)(2,1)S(1)} %get-tuple-element.98) | copy-start | bytes 3538948
  587.4 23.6 %slice-start.7 = ((s8[12189696]{0:T(1024)(128)(4,1)}), s8[4194304]{0:T(1024)(128)(4,1)S(1)}, s32[]{:S(2)}) async-start(s8[12189696]{0:T(1024)(128)(4,1)} %bitcast.416), calls=%async_computation.28 | async-start | bytes 8388608
  587.4 23.7 %slice-start.8 = ((s8[12189696]{0:T(1024)(128)(4,1)}), s8[4194304]{0:T(1024)(128)(4,1)S(1)}, s32[]{:S(2)}) async-start(s8[12189696]{0:T(1024)(128)(4,1)} %bitcast.416), calls=%async_computation.29 | async-start | bytes 8388608
  599.3 11.8 slice-start.9
  620.3 11.4 copy-start.56
  620.3 11.4 copy-start.12
  655.4 83.8 %copy-start.26 = (f32[384,1536]{1,0:T(8,128)}, f32[384,1536]{1,0:T(8,128)S(1)}, u32[]{:S(2)}) copy-start(f32[384,1536]{1,0:T(8,128)S(1)} %get-tuple-element.86) | copy-start | bytes 7077892
  655.4 83.8 %copy-start.30 = (f32[384,1536]{1,0:T(8,128)}, f32[384,1536]{1,0:T(8,128)S(1)}, u32[]{:S(2)}) copy-start(f32[384,1536]{1,0:T(8,128)S(1)} %get-tuple-element.87) | copy-start | bytes 7077892
  698.9 10.8 copy-start.55
  698.9 10.8 copy-start.54
  698.9 10.8 copy-start.92
  719.7 19.5 copy-start.86
  719.7 19.5 copy-start.87
  753.7 11.4 copy-start.44
  755.3 27.1 %copy-start.42 = (bf16[384,768]{0,1:T(8,128)(2,1)}, bf16[384,768]{0,1:T(8,128)(2,1)S(1)}, u32[]{:S(2)}) copy-start(bf16[384,768]{0,1:T(8,128)(2,1)S(1)} %copy.130) | copy-start | bytes 1769476
  764.7 404.4 %reduce-scatter.12.cloned.1.call-start = ((), (), s32[]{:S(2)}) async-start(), calls=%async_computation.16 | async-start | bytes 6488064 | tf_op jit(solution)/shard_map/reduce_scatter | solution.py:284
  822.4 346.6 %reduce-scatter.10.cloned.1.call-start = ((), (), s32[]{:S(2)}) async-start(), calls=%async_computation.15 | async-start | bytes 6488064 | tf_op jit(solution)/shard_map/reduce_scatter | solution.py:283
  829.9 408.8 %reduce-scatter.8.cloned.1.call-start = ((), (), s32[]{:S(2)}) async-start(), calls=%async_computation.14 | async-start | bytes 6488064 | tf_op jit(solution)/shard_map/reduce_scatter | solution.py:282
  837.3 14.5 copy-start.27
  837.3 652.9 %reduce-scatter.20.cloned.1.call-start = ((), (), s32[]{:S(2)}) async-start(), calls=%async_computation.20 | async-start | bytes 25952256 | tf_op jit(solution)/shard_map/reduce_scatter | solution.py:289
  926.7 14.8 copy-start.25
  926.7 816.7 %reduce-scatter.18.cloned.1.call-start = ((), (), s32[]{:S(2)}) async-start(), calls=%async_computation.19 | async-start | bytes 25952256 | tf_op jit(solution)/shard_map/reduce_scatter | solution.py:288
  1016.0 979.3 %reduce-scatter.16.cloned.1.call-start = ((), (), s32[]{:S(2)}) async-start(), calls=%async_computation.18 | async-start | bytes 25952256 | tf_op jit(solution)/shard_map/reduce_scatter | solution.py:287
  1113.6 47.2 %copy-start.88 = (f32[384]{0:T(512)S(1)}, f32[384]{0:T(512)}, u32[]{:S(2)}) copy-start(f32[384]{0:T(512)} %get-tuple-element.60) | copy-start | bytes 4612
  1113.6 47.2 %copy-start.65 = (bf16[1,384,1536]{2,1,0:T(8,128)(2,1)S(1)}, bf16[1,384,1536]{2,1,0:T(8,128)(2,1)}, u32[]{:S(2)}) copy-start(bf16[1,384,1536]{2,1,0:T(8,128)(2,1)} %get-tuple-element.92) | copy-start | bytes 3538948
  1113.6 50.3 %copy-start.18 = (f32[384,1536]{1,0:T(8,128)S(1)}, f32[384,1536]{1,0:T(8,128)}, u32[]{:S(2)}) copy-start(f32[384,1536]{1,0:T(8,128)} %copy-done.17) | copy-start | bytes 7077892
  1113.6 50.3 %copy-start.73 = (f32[1536]{0:T(1024)S(1)}, f32[1536]{0:T(1024)}, u32[]{:S(2)}) copy-start(f32[1536]{0:T(1024)} %convert_element_type.225) | copy-start | bytes 18436
  1113.6 50.3 %copy-start.81 = (f32[384]{0:T(512)S(1)}, f32[384]{0:T(512)}, u32[]{:S(2)}) copy-start(f32[384]{0:T(512)} %get-tuple-element.125) | copy-start | bytes 4612
  1167.4 827.9 %copy-start.1 = (bf16[32,12]{0,1:T(8,128)(2,1)S(1)}, bf16[32,12]{0,1:T(8,128)(2,1)}, u32[]{:S(2)}) copy-start(bf16[32,12]{0,1:T(8,128)(2,1)} %param.31) | copy-start | bytes 2308
  (69 other events, 285.0 us)
Sparse Core Ops, SparseCore 0:
  11.0 61.7 all-gather.9
  75.6 57.9 all-gather.11
  136.5 57.8 all-gather.7
  197.1 57.8 all-gather.13
  257.8 94.7 all-gather.15
  355.4 94.2 all-gather.17
  452.6 94.2 all-gather.19
  764.8 112.5 reduce-scatter.13
  884.5 113.8 reduce-scatter.11
  1004.5 113.5 reduce-scatter.9
  1125.2 113.4 reduce-scatter.7
  1245.6 244.6 reduce-scatter.19
  1498.4 245.0 reduce-scatter.17
  1750.3 245.0 reduce-scatter.15
where the time goes:
time: 2020 us; the launch traced here: 2000 us
  waiting for transfers between devices  1080 us (53%)
  local copies, waits for them, and re-layouts  382 us (19%)
  matrix products  356 us (18%)
  blocking collectives  123 us (6%)
  other arithmetic  41 us (2%)
    reduce_scatter x1, waiting for transfers between devices, body(): lax.psum_scatter(totals[7], ('fsdp', 'dp'), scatter_dimension=0, tiled=True)  253 us
    reduce_scatter x1, waiting for transfers between devices, body(): lax.psum_scatter(totals[6], ('fsdp', 'dp'), scatter_dimension=0, tiled=True)  252 us
    reduce_scatter x1, waiting for transfers between devices, body(): lax.psum_scatter(totals[8], ('fsdp', 'dp'), scatter_dimension=0, tiled=True)  252 us
    add x6, local copies, waits for them, and re-layouts, body(): jax.tree.map(jnp.add, totals, step_set)  173 us
    dot_general x14, matrix products, over_tokens(): lax.dot_general(former, latter, (((0,), (0,)), ((), ())), preferred_eleme...  122 us
    dot_general x14, matrix products, times_rows(): return jnp.dot(former, latter, preferred_element_type=jnp.float32)  104 us
    reshape x7, local copies, waits for them, and re-layouts, assemble(): jnp.transpose(shaped, (0, 2, 1, 3))  99.8 us
    dot_general x14, matrix products, times_transpose(): lax.dot_general(former, latter, (((1,), (1,)), ((), ())), preferred_eleme...  84 us
  transfers between devices with their start and end apart: 14, of which 10 were waited for; matrix products, arithmetic and copies ran while one was open for 27% of the time, Pallas kernels for 0%

commit v1 on v0

--- a/solution.py
+++ b/solution.py
@@ -129,12 +129,27 @@
         allowed = (block_ids[None, :] <= block_ids[:, None]) & (
             valid_mask[step_index, 0][None, :] == 1
         ) | diagonal
+
+        def _form_sums_all(here_x, dim_i):
+            after = lax.axis_index(("fsdp", "dp"))
+            y2 = lax.axis_size(("fsdp", "dp"))
+            passed, side_arr, all_values = (y2, after, here_x.shape[dim_i])
+            block_out, before = (here_x, 1)
+            while before < passed:
+                last = lax.ppermute(
+                    block_out, ("fsdp", "dp"), [(w, (w - before) % passed) for w in range(passed)]
+                )
+                block_out = jnp.concatenate([block_out, last], axis=dim_i)
+                before = 2 * before
+            earlier = jnp.roll(block_out, side_arr * all_values, axis=dim_i)
+            return earlier
+
         first_block = rebuild(
             (
                 lax.all_gather(first_gain, ("fsdp", "dp"), axis=0, tiled=True),
                 lax.all_gather(query_weight, ("fsdp", "dp"), axis=0, tiled=True),
                 lax.all_gather(key_weight, ("fsdp", "dp"), axis=0, tiled=True),
-                lax.all_gather(value_weight, ("fsdp", "dp"), axis=0, tiled=True),
+                _form_sums_all(value_weight, 0),
                 lax.all_gather(output_weight, ("fsdp", "dp"), axis=0, tiled=True),
             )
         )

time: 2020 us -> 2110 us (1.045)
  blocking collectives: 123 us -> 162 us
    reduce_scatter x1, waiting for transfers between devices: 0.01 us -> 117 us  [body(): lax.psum_scatter(totals[4], ('fsdp', 'dp'), scatter_dimension=0, tiled=True)]
    reduce_scatter x1, waiting for transfers between devices: 69.7 us -> 0.01 us  [body(): lax.psum_scatter(totals[1], ('fsdp', 'dp'), scatter_dimension=0, tiled=True)]
    all_gather x1, waiting for transfers between devices: 49.1 us -> 0.02 us  [body(): lax.all_gather(output_weight, ('fsdp', 'dp'), axis=0, tiled=True)]
    psum x1, blocking collectives: 42.2 us -> 81.8 us  [body(): valid_total = lax.psum(jnp.sum(valid_float), ('fsdp', 'dp'))]
    all_gather x1, waiting for transfers between devices: 24.9 us -> 58.7 us  [body(): lax.all_gather(gate_weight, ('fsdp', 'dp'), axis=0, tiled=True)]
    ppermute x0 -> x5, waiting for transfers between devices: none -> 31.7 us  [_form_sums_all(): lax.ppermute(block_out, ('fsdp', 'dp'), [(w, (w - before) % passed) for w...]
    all_gather x1, waiting for transfers between devices: 49.3 us -> 22.7 us  [body(): lax.all_gather(value_weight, ('fsdp', 'dp'), axis=0, tiled=True)]
    reshape x7 -> x8, local copies, waits for them, and re-layouts: 68.8 us -> 77 us  [assemble(): shaped = gathered.reshape(fsdp_count, dp_count, row_block, col_block)]
  transfers between devices with their start and end apart: 14 -> 19, of which waited for: 10 -> 12; matrix products, arithmetic and copies ran while one was open for 27% -> 25% of each run, Pallas kernels for 0% -> 0%
where the time goes in v1:
time: 2110 us; the launch traced here: 2100 us
  waiting for transfers between devices  1100 us (52%)
  local copies, waits for them, and re-layouts  403 us (19%)
  matrix products  359 us (17%)
  blocking collectives  162 us (8%)
  other arithmetic  41.7 us (2%)
    reduce_scatter x1, waiting for transfers between devices, body(): lax.psum_scatter(totals[7], ('fsdp', 'dp'), scatter_dimension=0, tiled=True)  253 us
    reduce_scatter x1, waiting for transfers between devices, body(): lax.psum_scatter(totals[8], ('fsdp', 'dp'), scatter_dimension=0, tiled=True)  252 us
    reduce_scatter x1, waiting for transfers between devices, body(): lax.psum_scatter(totals[6], ('fsdp', 'dp'), scatter_dimension=0, tiled=True)  252 us
    add x6, local copies, waits for them, and re-layouts, body(): jax.tree.map(jnp.add, totals, step_set)  173 us
    dot_general x14, matrix products, over_tokens(): lax.dot_general(former, latter, (((0,), (0,)), ((), ())), preferred_eleme...  122 us
    reduce_scatter x1, waiting for transfers between devices, body(): lax.psum_scatter(totals[4], ('fsdp', 'dp'), scatter_dimension=0, tiled=True)  117 us
    reshape x8, local copies, waits for them, and re-layouts, assemble(): jnp.transpose(shaped, (0, 2, 1, 3))  106 us
    dot_general x14, matrix products, times_rows(): return jnp.dot(former, latter, preferred_element_type=jnp.float32)  100 us
  transfers between devices with their start and end apart: 19, of which 12 were waited for; matrix products, arithmetic and copies ran while one was open for 25% of the time, Pallas kernels for 0%

profile of v1, /device:TPU:0, one launch (start us, length us, event | category | flops | bytes accessed | tf_op | source)
XLA Modules:
  0.0 2104.0 jit_solution(17442927298840282940)
XLA Ops:
  13.0 6.4 collective-permute-start
  27.6 7.6 collective-permute-done.2
  40.6 16.9 collective-permute-done.3
  62.4 81.8 %psum.22 = f32[]{:T(128)} all-reduce(f32[]{:T(128)} %convert_reduce_fusion), channel_id=1, replica_groups=mesh['fsdp'=8,'dp'=4] {'fsdp','dp'}, use_global_device_ids=true, to_apply=%region_12.14 | all-reduce | flops 1 | bytes 8 | tf_op jit(solution)/shard_map/psum | solution.py:94
  144.7 40.8 %all-reduce.5 = (bf16[1536]{0:T(1024)(128)(2,1)S(1)}, bf16[1536]{0:T(1024)(128)(2,1)S(1)}) all-reduce(bf16[1536]{0:T(1024)(128)(2,1)S(1)} %dynamic-update-slice, bf16[1536]{0:T(1024)(128)(2,1)S(1)} %dynamic-update-slice.1), channel_id=1, replica_groups=mesh['fsdp'=8,'dp'=4] {'fsdp','dp'}, use_global_device_ids=true, to_apply=%add | all-reduce | flops 3072 | bytes 12288
  204.6 7.5 reshape.535
  285.0 22.7 %all-gather.20.cloned.1.call-done = bf16[6144,192]{1,0:T(8,128)(2,1)} async-done(((bf16[192,192]{1,0:T(8,128)(2,1)}), bf16[6144,192]{1,0:T(8,128)(2,1)}) %all-gather.20.cloned.1.call-update) | async-done | bytes 2359312 | tf_op jit(solution)/shard_map/all_gather | solution.py:228
  319.6 7.5 fusion.121
  346.6 58.7 %all-gather.14.cloned.1.call-done = bf16[6144,992]{1,0:T(8,128)(2,1)} async-done(((bf16[192,992]{1,0:T(8,128)(2,1)}), bf16[6144,992]{1,0:T(8,128)(2,1)}) %all-gather.14.cloned.1.call-update) | async-done | bytes 12189712 | tf_op jit(solution)/shard_map/all_gather | solution.py:180
  405.3 15.7 copy.223
  421.0 25.0 %reshape.548 = bf16[1536,3968]{1,0:T(8,128)(2,1)} reshape(bf16[8,192,4,992]{3,2,1,0:T(4,128)(2,1)} %bitcast.403) | data formatting | bytes 24379392 | tf_op jit(solution)/shard_map/reshape | solution.py:31
  446.0 56.4 %all-gather.16.cloned.1.call-done = bf16[6144,992]{1,0:T(8,128)(2,1)} async-done(((bf16[192,992]{1,0:T(8,128)(2,1)}), bf16[6144,992]{1,0:T(8,128)(2,1)}) %all-gather.16.cloned.1.call-update) | async-done | bytes 12189712 | tf_op jit(solution)/shard_map/all_gather | solution.py:181
  502.3 15.6 copy.222
  518.0 25.0 %reshape.550 = bf16[1536,3968]{1,0:T(8,128)(2,1)} reshape(bf16[8,192,4,992]{3,2,1,0:T(4,128)(2,1)} %bitcast.404) | data formatting | bytes 24379392 | tf_op jit(solution)/shard_map/reshape | solution.py:31
  543.0 56.5 %all-gather.18.cloned.1.call-done = bf16[6144,992]{1,0:T(8,128)(2,1)} async-done(((bf16[192,992]{1,0:T(8,128)(2,1)}), bf16[6144,992]{1,0:T(8,128)(2,1)}) %all-gather.18.cloned.1.call-update) | async-done | bytes 12189712 | tf_op jit(solution)/shard_map/all_gather | solution.py:182
  599.5 15.6 copy.221
  615.1 25.0 %reshape.552 = bf16[1536,3968]{1,0:T(8,128)(2,1)} reshape(bf16[8,192,4,992]{3,2,1,0:T(4,128)(2,1)} %bitcast.405) | data formatting | bytes 24379392 | tf_op jit(solution)/shard_map/reshape | solution.py:31
  640.1 11.8 fusion.123
  651.9 12.3 fusion.122
  664.2 9.2 multiply_convert_fusion.4
  673.5 10.8 multiply_convert_fusion.5
  684.3 9.9 convolution_add_fusion.11
  694.2 13.6 fusion.74
  707.9 17.3 multiply_convert_fusion.3
  725.1 11.1 fusion.124
  736.2 15.5 multiply_convert_fusion.2
  751.7 11.1 fusion.126
  762.9 9.9 convolution_add_fusion.10
  772.8 19.3 multiply_reduce_fusion.2
  802.0 7.7 multiply_reduce_fusion.1
  825.4 7.6 multiply_reduce_fusion
  892.1 13.7 fusion.132
  905.8 17.5 convolution_add_fusion.2
  923.3 32.5 %add.295 = f32[8,192,4,992]{3,2,1,0:T(4,128)} reshape(f32[1536,3968]{1,0:T(8,128)} %convolution_add_fusion.2) | data formatting | bytes 48758784 | tf_op jit(solution)/shard_map/add | solution.py:294
  955.9 25.0 %copy.184 = f32[8,4,192,992]{3,2,1,0:T(8,128)} copy(f32[8,4,192,992]{3,1,2,0:T(4,128)} %bitcast.400) | data formatting | bytes 48758784 | tf_op jit(solution)/shard_map/add | solution.py:294
  981.1 13.7 fusion.133
  994.8 17.8 convolution_add_fusion.1
  1012.6 32.6 %add.299 = f32[8,192,4,992]{3,2,1,0:T(4,128)} reshape(f32[1536,3968]{1,0:T(8,128)} %convolution_add_fusion.1) | data formatting | bytes 48758784 | tf_op jit(solution)/shard_map/add | solution.py:294
  1045.2 25.1 %copy.185 = f32[8,4,192,992]{3,2,1,0:T(8,128)} copy(f32[8,4,192,992]{3,1,2,0:T(4,128)} %bitcast.401) | data formatting | bytes 48758784 | tf_op jit(solution)/shard_map/add | solution.py:294
  1070.6 13.9 fusion.107
  1084.5 17.0 convolution_add_fusion
  1101.5 32.8 %add.303 = f32[8,192,4,992]{3,2,1,0:T(4,128)} reshape(f32[1536,3968]{1,0:T(8,128)} %convolution_add_fusion) | data formatting | bytes 48758784 | tf_op jit(solution)/shard_map/add | solution.py:294
  1134.2 25.3 %copy.186 = f32[8,4,192,992]{3,2,1,0:T(8,128)} copy(f32[8,4,192,992]{3,1,2,0:T(4,128)} %bitcast.402) | data formatting | bytes 48758784 | tf_op jit(solution)/shard_map/add | solution.py:294
  1170.9 39.4 %all-reduce.4 = (f32[]{:T(128)}, f32[1536]{0:T(1024)}, f32[1536]{0:T(1024)}, f32[32,12]{0,1:T(8,128)}) all-reduce(f32[]{:T(128)S(6)} %add.265, f32[1536]{0:T(1024)} %add.280, f32[1536]{0:T(1024)} %add.293, f32[32,12]{0,1:T(8,128)} %fusion.99), channel_id=1, replica_groups=mesh['fsdp'=8,'dp'=4] {'fsdp','dp'}, use_global_device_ids=true, to_apply=%region_10.12 | all-reduce | flops 3457 | bytes 27656 | tf_op jit(solution)/shard_map/psum | solution.py:306
  1222.0 117.4 %reduce-scatter.14.cloned.1.call-done = f32[192,192]{1,0:T(8,128)} async-done(((f32[6144,192]{1,0:T(8,128)}), f32[192,192]{1,0:T(8,128)}) %reduce-scatter.14.cloned.1.call-update) | async-done | bytes 147472 | tf_op jit(solution)/shard_map/reduce_scatter | solution.py:300
  1339.5 251.5 %reduce-scatter.16.cloned.1.call-done = f32[192,992]{1,0:T(8,128)} async-done(((f32[6144,992]{1,0:T(8,128)}), f32[192,992]{1,0:T(8,128)}) %reduce-scatter.16.cloned.1.call-update) | async-done | bytes 761872 | tf_op jit(solution)/shard_map/reduce_scatter | solution.py:302
  1591.0 253.2 %reduce-scatter.18.cloned.1.call-done = f32[192,992]{1,0:T(8,128)} async-done(((f32[6144,992]{1,0:T(8,128)}), f32[192,992]{1,0:T(8,128)}) %reduce-scatter.18.cloned.1.call-update) | async-done | bytes 761872 | tf_op jit(solution)/shard_map/reduce_scatter | solution.py:303
  1844.1 251.9 %reduce-scatter.20.cloned.1.call-done = f32[192,992]{1,0:T(8,128)} async-done(((f32[6144,992]{1,0:T(8,128)}), f32[192,992]{1,0:T(8,128)}) %reduce-scatter.20.cloned.1.call-update) | async-done | bytes 761872 | tf_op jit(solution)/shard_map/reduce_scatter | solution.py:304
  (359 shorter events, 252.4 us)
Async XLA Ops:
  7.2 182.5 %copy-start = (bf16[32,12]{0,1:T(8,128)(2,1)S(1)}, bf16[32,12]{0,1:T(8,128)(2,1)}, u32[]{:S(2)}) copy-start(bf16[32,12]{0,1:T(8,128)(2,1)} %param.33) | copy-start | bytes 2308
  7.2 32.8 %copy-start.75 = (s32[2,1,384]{2,1,0:T(1,128)S(1)}, s32[2,1,384]{2,1,0:T(1,128)}, u32[]{:S(2)}) copy-start(s32[2,1,384]{2,1,0:T(1,128)} %param.21) | copy-start | bytes 9220
  7.2 32.8 %copy-start.90 = (s32[2,1,384]{2,1,0:T(1,128)S(1)}, s32[2,1,384]{2,1,0:T(1,128)}, u32[]{:S(2)}) copy-start(s32[2,1,384]{2,1,0:T(1,128)} %param.22) | copy-start | bytes 9220
  7.2 222.6 %all-gather.8.cloned.1.call-start = ((), (), s32[]{:S(2)}) async-start(), calls=%async_computation.7 | async-start | bytes 3244032 | tf_op jit(solution)/shard_map/all_gather | solution.py:150
  7.9 236.9 %all-gather.10.cloned.1.call-start = ((), (), s32[]{:S(2)}) async-start(), calls=%async_computation.8 | async-start | bytes 3244032 | tf_op jit(solution)/shard_map/all_gather | solution.py:151
  8.7 253.0 %all-gather.12.cloned.1.call-start = ((), (), s32[]{:S(2)}) async-start(), calls=%async_computation.9 | async-start | bytes 3244032 | tf_op jit(solution)/shard_map/all_gather | solution.py:153
  9.4 298.3 %all-gather.20.cloned.1.call-start = ((), (), s32[]{:S(2)}) async-start(), calls=%async_computation.13 | async-start | bytes 3244032 | tf_op jit(solution)/shard_map/all_gather | solution.py:228
  10.0 395.3 %all-gather.14.cloned.1.call-start = ((), (), s32[]{:S(2)}) async-start(), calls=%async_computation.10 | async-start | bytes 12976128 | tf_op jit(solution)/shard_map/all_gather | solution.py:180
  10.6 491.7 %all-gather.16.cloned.1.call-start = ((), (), s32[]{:S(2)}) async-start(), calls=%async_computation.11 | async-start | bytes 12976128 | tf_op jit(solution)/shard_map/all_gather | solution.py:181
  11.2 588.3 %all-gather.18.cloned.1.call-start = ((), (), s32[]{:S(2)}) async-start(), calls=%async_computation.12 | async-start | bytes 12976128 | tf_op jit(solution)/shard_map/all_gather | solution.py:182
  11.9 1210.1 %reduce-scatter.8.cloned.1.call-start = ((), (), s32[]{:S(2)}) async-start(), calls=%async_computation.14 | async-start | bytes 6488064 | tf_op jit(solution)/shard_map/reduce_scatter | solution.py:297
  13.0 131.3 %copy-start.93 = (bf16[48]{0:T(256)(128)(2,1)S(1)}, bf16[48]{0:T(256)(128)(2,1)}, u32[]{:S(2)}) copy-start(bf16[48]{0:T(256)(128)(2,1)} %param.24) | copy-start | bytes 292
  13.0 131.5 %copy-start.94 = (bf16[48]{0:T(256)(128)(2,1)S(1)}, bf16[48]{0:T(256)(128)(2,1)}, u32[]{:S(2)}) copy-start(bf16[48]{0:T(256)(128)(2,1)} %param.29) | copy-start | bytes 292
  13.0 8.6 collective-permute-start
  21.7 5.6 collective-permute-start.1
  27.4 158.1 %copy-start.58 = (bf16[384,192]{0,1:T(8,128)(2,1)}, bf16[384,192]{0,1:T(8,128)(2,1)S(1)}, u32[]{:S(2)}) copy-start(bf16[384,192]{0,1:T(8,128)(2,1)S(1)} %collective-permute-done.1) | copy-start | bytes 442372
  27.5 160.0 %copy-start.4 = (bf16[2,1,384,1536]{3,2,1,0:T(8,128)(2,1)S(1)}, bf16[2,1,384,1536]{3,2,1,0:T(8,128)(2,1)}, u32[]{:S(2)}) copy-start(bf16[2,1,384,1536]{3,2,1,0:T(8,128)(2,1)} %param.18) | copy-start | bytes 7077892
  27.5 7.7 collective-permute-start.2
  36.2 21.3 %collective-permute-start.3 = (bf16[1536,192]{0,1:T(8,128)(2,1)}, bf16[1536,192]{0,1:T(8,128)(2,1)}, u32[]{:S(2)}, u32[]{:S(2)}) collective-permute-start(bf16[1536,192]{0,1:T(8,128)(2,1)} %concatenate.33), channel_id=1, source_target_pairs={{0,24},{1,25},{2,26},{3,27},{4,28},{5,29},{6,30},{7,31},{8,0},{9,1... | collective-permute-start | bytes 1769480 | tf_op jit(solution)/shard_map/ppermute | solution.py:139
  60.6 134.4 %collective-permute-start.4 = (bf16[3072,192]{0,1:T(8,128)(2,1)}, bf16[3072,192]{0,1:T(8,128)(2,1)}, u32[]{:S(2)}, u32[]{:S(2)}) collective-permute-start(bf16[3072,192]{0,1:T(8,128)(2,1)} %concatenate.34), channel_id=1, source_target_pairs={{0,16},{1,17},{2,18},{3,19},{4,20},{5,21},{6,22},{7,23},{8,24},{9,... | collective-permute-start | bytes 3538952 | tf_op jit(solution)/shard_map/ppermute | solution.py:139
  185.5 40.4 %copy-start.69 = (f32[1536]{0:T(1024)}, f32[1536]{0:T(1024)S(1)}, u32[]{:S(2)}) copy-start(f32[1536]{0:T(1024)S(1)} %convert_element_type.225) | copy-start | bytes 18436
  186.8 159.3 %copy-start.67 = (f32[1536]{0:T(1024)}, f32[1536]{0:T(1024)S(1)}, u32[]{:S(2)}) copy-start(f32[1536]{0:T(1024)S(1)} %convert_element_type.234) | copy-start | bytes 18436
  188.7 37.2 %copy-start.79 = (f32[384]{0:T(512)}, f32[384]{0:T(512)S(1)}, u32[]{:S(2)}) copy-start(f32[384]{0:T(512)S(1)} %get-tuple-element.139) | copy-start | bytes 4612
  188.7 68.0 %copy-start.76 = (f32[384]{0:T(512)}, f32[384]{0:T(512)S(1)}, u32[]{:S(2)}) copy-start(f32[384]{0:T(512)S(1)} %get-tuple-element.117) | copy-start | bytes 4612
  244.9 89.9 %copy-start.36 = (bf16[384,768]{0,1:T(8,128)(2,1)}, bf16[384,768]{0,1:T(8,128)(2,1)S(1)}, u32[]{:S(2)}) copy-start(bf16[384,768]{0,1:T(8,128)(2,1)S(1)} %copy.168) | copy-start | bytes 1769476
  261.7 73.1 %copy-start.38 = (bf16[384,768]{0,1:T(8,128)(2,1)}, bf16[384,768]{0,1:T(8,128)(2,1)S(1)}, u32[]{:S(2)}) copy-start(bf16[384,768]{0,1:T(8,128)(2,1)S(1)} %copy.169) | copy-start | bytes 1769476
  346.6 317.6 %copy-start.24 = (bf16[384,1536]{1,0:T(8,128)(2,1)}, bf16[384,1536]{1,0:T(8,128)(2,1)S(1)}, u32[]{:S(2)}) copy-start(bf16[384,1536]{1,0:T(8,128)(2,1)S(1)} %get-tuple-element.113) | copy-start | bytes 3538948
  346.6 326.9 %copy-start.28 = (bf16[384,1536]{1,0:T(8,128)(2,1)}, bf16[384,1536]{1,0:T(8,128)(2,1)S(1)}, u32[]{:S(2)}) copy-start(bf16[384,1536]{1,0:T(8,128)(2,1)S(1)} %get-tuple-element.112) | copy-start | bytes 3538948
  640.1 24.1 %slice-start.7 = ((s8[12189696]{0:T(1024)(128)(4,1)}), s8[4194304]{0:T(1024)(128)(4,1)S(1)}, s32[]{:S(2)}) async-start(s8[12189696]{0:T(1024)(128)(4,1)} %bitcast.424), calls=%async_computation.28 | async-start | bytes 8388608
  640.1 24.1 %slice-start.8 = ((s8[12189696]{0:T(1024)(128)(4,1)}), s8[4194304]{0:T(1024)(128)(4,1)S(1)}, s32[]{:S(2)}) async-start(s8[12189696]{0:T(1024)(128)(4,1)} %bitcast.424), calls=%async_computation.29 | async-start | bytes 8388608
  707.8 84.3 %copy-start.26 = (f32[384,1536]{1,0:T(8,128)}, f32[384,1536]{1,0:T(8,128)S(1)}, u32[]{:S(2)}) copy-start(f32[384,1536]{1,0:T(8,128)S(1)} %get-tuple-element.100) | copy-start | bytes 7077892
  725.1 37.7 %copy-start.53 = (bf16[384,3968]{1,0:T(8,128)(2,1)}, bf16[384,3968]{1,0:T(8,128)(2,1)S(1)}, u32[]{:S(2)}) copy-start(bf16[384,3968]{1,0:T(8,128)(2,1)S(1)} %get-tuple-element.98) | copy-start | bytes 9142276
  751.7 21.1 %copy-start.55 = (bf16[384,3968]{1,0:T(8,128)(2,1)}, bf16[384,3968]{1,0:T(8,128)(2,1)S(1)}, u32[]{:S(2)}) copy-start(bf16[384,3968]{1,0:T(8,128)(2,1)S(1)} %get-tuple-element.96) | copy-start | bytes 9142276
  772.8 19.4 copy-start.31
  772.8 19.4 copy-start.87
  772.8 19.4 copy-start.88
  865.2 356.8 %reduce-scatter.10.cloned.1.call-start = ((), (), s32[]{:S(2)}) async-start(), calls=%async_computation.15 | async-start | bytes 6488064 | tf_op jit(solution)/shard_map/reduce_scatter | solution.py:298
  873.0 349.0 %reduce-scatter.12.cloned.1.call-start = ((), (), s32[]{:S(2)}) async-start(), calls=%async_computation.16 | async-start | bytes 6488064 | tf_op jit(solution)/shard_map/reduce_scatter | solution.py:299
  880.5 459.0 %reduce-scatter.14.cloned.1.call-start = ((), (), s32[]{:S(2)}) async-start(), calls=%async_computation.17 | async-start | bytes 6488064 | tf_op jit(solution)/shard_map/reduce_scatter | solution.py:300
  890.8 700.1 %reduce-scatter.16.cloned.1.call-start = ((), (), s32[]{:S(2)}) async-start(), calls=%async_computation.18 | async-start | bytes 25952256 | tf_op jit(solution)/shard_map/reduce_scatter | solution.py:302
  980.9 863.3 %reduce-scatter.18.cloned.1.call-start = ((), (), s32[]{:S(2)}) async-start(), calls=%async_computation.19 | async-start | bytes 25952256 | tf_op jit(solution)/shard_map/reduce_scatter | solution.py:303
  1070.4 1025.7 %reduce-scatter.20.cloned.1.call-start = ((), (), s32[]{:S(2)}) async-start(), calls=%async_computation.20 | async-start | bytes 25952256 | tf_op jit(solution)/shard_map/reduce_scatter | solution.py:304
  1167.6 46.5 %copy-start.89 = (f32[384]{0:T(512)S(1)}, f32[384]{0:T(512)}, u32[]{:S(2)}) copy-start(f32[384]{0:T(512)} %get-tuple-element.74) | copy-start | bytes 4612
  1167.6 46.5 %copy-start.62 = (bf16[1,384,1536]{2,1,0:T(8,128)(2,1)S(1)}, bf16[1,384,1536]{2,1,0:T(8,128)(2,1)}, u32[]{:S(2)}) copy-start(bf16[1,384,1536]{2,1,0:T(8,128)(2,1)} %get-tuple-element.106) | copy-start | bytes 3538948
  1167.6 49.6 %copy-start.18 = (f32[384,1536]{1,0:T(8,128)S(1)}, f32[384,1536]{1,0:T(8,128)}, u32[]{:S(2)}) copy-start(f32[384,1536]{1,0:T(8,128)} %copy-done.17) | copy-start | bytes 7077892
  1167.7 49.6 %copy-start.73 = (f32[1536]{0:T(1024)S(1)}, f32[1536]{0:T(1024)}, u32[]{:S(2)}) copy-start(f32[1536]{0:T(1024)} %copy-done.69) | copy-start | bytes 18436
  1167.7 49.6 %copy-start.82 = (f32[384]{0:T(512)S(1)}, f32[384]{0:T(512)}, u32[]{:S(2)}) copy-start(f32[384]{0:T(512)} %copy-done.79) | copy-start | bytes 4612
  1220.4 875.6 %copy-start.1 = (bf16[32,12]{0,1:T(8,128)(2,1)S(1)}, bf16[32,12]{0,1:T(8,128)(2,1)}, u32[]{:S(2)}) copy-start(bf16[32,12]{0,1:T(8,128)(2,1)} %param.33) | copy-start | bytes 2308
  (77 other events, 390.9 us)
Sparse Core Ops, SparseCore 0:
  10.9 94.3 all-gather.7
  108.2 78.1 all-gather.9
  189.2 57.7 all-gather.11
  249.8 57.8 all-gather.19
  310.5 94.8 all-gather.13
  408.1 94.2 all-gather.15
  505.2 94.2 all-gather.17
  865.3 112.6 reduce-scatter.7
  985.1 113.5 reduce-scatter.9
  1104.8 114.2 reduce-scatter.11
  1226.2 113.2 reduce-scatter.13
  1346.3 244.6 reduce-scatter.15
  1599.1 245.0 reduce-scatter.17
  1851.0 244.9 reduce-scatter.19
